TPU v7x, 32 devices: a whole 2x2x4 slice. The times are simulated.
32 devices in a mesh: dp: 16 (over z, y, core), fsdp: 2 (over x).
Axes of the slice: x: 2, y: 2, z: 4, core: 2. Of those that a mesh axis runs over, the one named last changes fastest.
Arguments:
- hidden_in: bfloat16 [4096, 1024], P(('dp', 'fsdp')), may hold values from -6 to 6
- doc_id: int32 [4096], P(('dp', 'fsdp')), may hold values from 0 to 128, as said below
- expert_ids: int32 [4096, 8], P(('dp', 'fsdp')), may hold values from 0 to 15, all different within a row
- out_grad: bfloat16 [4096, 1024], P(('dp', 'fsdp')), may hold values from -6 to 6
- attn_gain: bfloat16 [1024], P(('dp', 'fsdp')), may hold values from 0.5 to 1.5
- query_weight: bfloat16 [1024, 1024], P(('dp', 'fsdp')), may hold values from -0.1875 to 0.1875
- key_weight: bfloat16 [1024, 512], P(('dp', 'fsdp')), may hold values from -0.1875 to 0.1875
- value_weight: bfloat16 [1024, 512], P(('dp', 'fsdp')), may hold values from -0.1875 to 0.1875
- output_weight: bfloat16 [1024, 1024], P(('dp', 'fsdp')), may hold values from -0.75 to 0.75
- ffn_gain: bfloat16 [1024], P(('dp', 'fsdp')), may hold values from 0.5 to 1.5
- router_weight: bfloat16 [1024, 16], P(('dp', 'fsdp')), may hold values from -0.375 to 0.375
- expert_gate: bfloat16 [16, 1024, 512], P('dp', 'fsdp'), may hold values from -0.1875 to 0.1875
- expert_up: bfloat16 [16, 1024, 512], P('dp', 'fsdp'), may hold values from -0.1875 to 0.1875
- expert_down: bfloat16 [16, 512, 1024], P('dp', 'fsdp'), may hold values from -1 to 1
Outputs:
- layer_out: bfloat16 [4096, 1024], P(('dp', 'fsdp'))
- grad_in: bfloat16 [4096, 1024], P(('dp', 'fsdp'))
- grad_attn_gain: float32 [1024], P(('dp', 'fsdp'))
- grad_query: float32 [1024, 1024], P(('dp', 'fsdp'))
- grad_key: float32 [1024, 512], P(('dp', 'fsdp'))
- grad_value: float32 [1024, 512], P(('dp', 'fsdp'))
- grad_output: float32 [1024, 1024], P(('dp', 'fsdp'))
- grad_ffn_gain: float32 [1024], P(('dp', 'fsdp'))
- grad_router: float32 [1024, 16], P(('dp', 'fsdp'))
- grad_expert_gate: float32 [16, 1024, 512], P('dp', 'fsdp')
- grad_expert_up: float32 [16, 1024, 512], P('dp', 'fsdp')
- grad_expert_down: float32 [16, 512, 1024], P('dp', 'fsdp')
Inputs may be any that keep to these rules, and one draw needn't show every extreme that they name: Within each block of 128 rows doc_id starts at 0 and never falls; live rows come first and carry ids below 128; the rows after them carry 128 (padding). Every block has 64 or more live rows and some block has no padding. `expert_ids`: each row names 8 different experts.
All inputs are finite; a program needn't handle non-finite values.
Results may differ from a plain program's by a relative error of at most 0.015.
The roundings to bfloat16 on the way count: a program that leaves them out, or rounds other values in their place, can miss the bound.
Values may be sent and summed in bfloat16 or wider, within the bound.
A program may use at most 128 MiB of HBM per device.

v0:
```python
import jax
import jax.numpy as jnp
from jax import lax
from jax.sharding import PartitionSpec as P

HEADS = 16
KV_HEADS = 8
HEAD_DIM = 64
TOP = 8
CAP = 24
norm_eps = 1e-05


def positions_mask(doc_block):
    row_count = doc_block.shape[0]
    row_index = jnp.arange(row_count)
    same_doc = doc_block[:, None] == doc_block[None, :]
    earlier = row_index[None, :] < row_index[:, None]
    position = jnp.sum((same_doc & earlier).astype(jnp.float32), axis=1)
    allowed = same_doc & (row_index[None, :] <= row_index[:, None])
    live_rows = (doc_block < row_count).astype(jnp.float32)
    return (position, allowed, live_rows)


def rope_tables(position):
    half_dim = HEAD_DIM // 2
    freqs = jnp.exp(-jnp.log(10000.0) * (2.0 * jnp.arange(half_dim, dtype=jnp.float32) / HEAD_DIM))
    angle = position[:, None] * freqs[None, :]
    return (jnp.cos(angle), jnp.sin(angle))


def rotate(values, cosine, sinusoid):
    half_dim = values.shape[-1] // 2
    first_half, second_half = (values[..., :half_dim], values[..., half_dim:])
    return jnp.concatenate(
        [
            first_half * cosine - second_half * sinusoid,
            second_half * cosine + first_half * sinusoid,
        ],
        axis=-1,
    )


def unrotate(values, cosine, sinusoid):
    half_dim = values.shape[-1] // 2
    first_half, second_half = (values[..., :half_dim], values[..., half_dim:])
    return jnp.concatenate(
        [
            first_half * cosine + second_half * sinusoid,
            second_half * cosine - first_half * sinusoid,
        ],
        axis=-1,
    )


def norm_forward(values, gain):
    scale_row = lax.rsqrt(jnp.mean(values * values, axis=-1, keepdims=True) + norm_eps)
    normed = values * scale_row
    return (normed, scale_row, (normed * gain).astype(jnp.bfloat16))


def norm_backward(upstream, normed, scale_row, gain):
    scaled = upstream * gain
    inner = jnp.mean(scaled * normed, axis=-1, keepdims=True)
    return (scale_row * (scaled - normed * inner), jnp.sum(upstream * normed, axis=0))


def probabilities(query_b, key_b, allowed, log_total):
    scores = jnp.einsum(
        "ikgd,jkd->kgij", query_b, key_b, preferred_element_type=jnp.float32
    ) * HEAD_DIM ** (-0.5)
    raised = jnp.where(allowed[None, None], jnp.exp(scores), 0.0)
    if log_total is None:
        log_total = jnp.log(jnp.sum(raised, axis=-1, keepdims=True))
    return (jnp.where(allowed[None, None], jnp.exp(scores - log_total), 0.0), log_total)


def routing(expert_block, live_rows, logits):
    experts = logits.shape[1]
    row_count = expert_block.shape[0]
    chosen = jnp.sum(
        (expert_block[:, :, None] == jnp.arange(experts)[None, None, :]).astype(jnp.float32), axis=1
    )
    raised = jnp.where(chosen > 0, jnp.exp(logits), 0.0)
    gates = raised / jnp.sum(raised, axis=1, keepdims=True)
    member = chosen * live_rows[:, None]
    lower = (jnp.arange(row_count)[None, :] < jnp.arange(row_count)[:, None]).astype(jnp.float32)
    rank = jnp.dot(lower, member, precision=lax.Precision.HIGHEST)
    kept = member * (rank < CAP).astype(jnp.float32)
    slot_match = (rank.T[:, None, :] == jnp.arange(CAP, dtype=jnp.float32)[None, :, None]).astype(
        jnp.float32
    )
    dispatch = kept.T[:, None, :] * slot_match
    return (gates, dispatch, kept, rank)


def expert_forward(rows_in, w_gate, w_up, w_down):
    gate_pre = jnp.dot(rows_in, w_gate, preferred_element_type=jnp.float32)
    up_pre = jnp.dot(rows_in, w_up, preferred_element_type=jnp.float32)
    act_rows = (jax.nn.silu(gate_pre) * up_pre).astype(jnp.bfloat16)
    out_rows = jnp.dot(act_rows, w_down, preferred_element_type=jnp.float32).astype(jnp.bfloat16)
    return (gate_pre, up_pre, act_rows, out_rows)


def expert_backward(rows_in, gate_pre, up_pre, act_rows, grad_rows, w_gate, w_up, w_down):
    grad_act = jnp.dot(grad_rows, w_down.T, preferred_element_type=jnp.float32)
    sigmoid_gate = jax.nn.sigmoid(gate_pre)
    grad_up_pre = (grad_act * gate_pre * sigmoid_gate).astype(jnp.bfloat16)
    grad_gate_pre = (
        grad_act * up_pre * sigmoid_gate * (1.0 + gate_pre * (1.0 - sigmoid_gate))
    ).astype(jnp.bfloat16)
    grad_down_w = jnp.dot(act_rows.T, grad_rows, preferred_element_type=jnp.float32)
    grad_gate_w = jnp.dot(rows_in.T, grad_gate_pre, preferred_element_type=jnp.float32)
    grad_up_w = jnp.dot(rows_in.T, grad_up_pre, preferred_element_type=jnp.float32)
    grad_rows_in = jnp.dot(grad_gate_pre, w_gate.T, preferred_element_type=jnp.float32)
    grad_rows_in = (
        grad_rows_in + jnp.dot(grad_up_pre, w_up.T, preferred_element_type=jnp.float32)
    ).astype(jnp.bfloat16)
    return (grad_rows_in, grad_gate_w, grad_up_w, grad_down_w)


def shards(
    hidden_in,
    doc_id,
    expert_ids,
    out_grad,
    attn_gain,
    query_weight,
    key_weight,
    value_weight,
    output_weight,
    ffn_gain,
    router_weight,
    expert_gate,
    expert_up,
    expert_down,
):
    rows = hidden_in.shape[0]
    groups = HEADS // KV_HEADS
    scale = HEAD_DIM ** (-0.5)
    dense_full = (
        lax.all_gather(attn_gain, ("dp", "fsdp"), axis=0, tiled=True),
        lax.all_gather(query_weight, ("dp", "fsdp"), axis=0, tiled=True),
        lax.all_gather(key_weight, ("dp", "fsdp"), axis=0, tiled=True),
        lax.all_gather(value_weight, ("dp", "fsdp"), axis=0, tiled=True),
        lax.all_gather(output_weight, ("dp", "fsdp"), axis=0, tiled=True),
        lax.all_gather(ffn_gain, ("dp", "fsdp"), axis=0, tiled=True),
        lax.all_gather(router_weight, ("dp", "fsdp"), axis=0, tiled=True),
    )
    expert_full = (
        lax.all_gather(expert_gate, "fsdp", axis=1, tiled=True),
        lax.all_gather(expert_up, "fsdp", axis=1, tiled=True),
        lax.all_gather(expert_down, "fsdp", axis=1, tiled=True),
    )
    gain_one, w_query, w_key, w_value, w_output, gain_two, w_router = dense_full
    w_gate, w_up, w_down = (expert_full[0][0], expert_full[1][0], expert_full[2][0])
    position, allowed, live_rows = positions_mask(doc_id)
    cosine, sinusoid = rope_tables(position)
    cos_query, sin_query = (cosine[:, None, None, :], sinusoid[:, None, None, :])
    cos_key, sin_key = (cosine[:, None, :], sinusoid[:, None, :])
    resid_in = hidden_in.astype(jnp.float32)
    normed_one, scale_one, normed_in = norm_forward(resid_in, gain_one.astype(jnp.float32))
    query_raw = jnp.dot(normed_in, w_query, preferred_element_type=jnp.float32).reshape(
        rows, KV_HEADS, groups, HEAD_DIM
    )
    key_raw = jnp.dot(normed_in, w_key, preferred_element_type=jnp.float32).reshape(
        rows, KV_HEADS, HEAD_DIM
    )
    query_b = rotate(query_raw, cos_query, sin_query).astype(jnp.bfloat16)
    key_b = rotate(key_raw, cos_key, sin_key).astype(jnp.bfloat16)
    value_b = (
        jnp.dot(normed_in, w_value, preferred_element_type=jnp.float32)
        .reshape(rows, KV_HEADS, HEAD_DIM)
        .astype(jnp.bfloat16)
    )
    probs, log_total = probabilities(query_b, key_b, allowed, None)
    probs_b = probs.astype(jnp.bfloat16)
    mixed = jnp.einsum("kgij,jkd->ikgd", probs_b, value_b, preferred_element_type=jnp.float32)
    mixed_b = (
        (mixed * live_rows[:, None, None, None])
        .reshape(rows, HEADS * HEAD_DIM)
        .astype(jnp.bfloat16)
    )
    resid_mid = resid_in + jnp.dot(mixed_b, w_output, preferred_element_type=jnp.float32)
    normed_two, scale_two, routed_in = norm_forward(resid_mid, gain_two.astype(jnp.float32))
    logits = jnp.dot(routed_in, w_router, preferred_element_type=jnp.float32)
    gates, dispatch, kept, rank = routing(expert_ids, live_rows, logits)
    dispatch_b = dispatch.astype(jnp.bfloat16)
    send_rows = jnp.einsum(
        "ecr,rd->ecd", dispatch_b, routed_in, preferred_element_type=jnp.float32
    ).astype(jnp.bfloat16)
    recv_rows = lax.all_to_all(send_rows, "dp", split_axis=0, concat_axis=0, tiled=True)
    flat_in = recv_rows.reshape(-1, recv_rows.shape[2])
    gate_pre, up_pre, act_rows, out_rows = expert_forward(flat_in, w_gate, w_up, w_down)
    back_rows = lax.all_to_all(
        out_rows.reshape(recv_rows.shape), "dp", split_axis=0, concat_axis=0, tiled=True
    )
    experts = back_rows.shape[0]
    capacity = back_rows.shape[1]
    width = back_rows.shape[2]
    chosen_slot = (expert_ids[:, :, None] == jnp.arange(experts)[None, None, :]).astype(jnp.float32)
    gate_pick = jnp.sum(chosen_slot * (gates * kept)[:, None, :], axis=2)
    rank_pick = jnp.sum(chosen_slot * rank[:, None, :], axis=2)
    slot_index = expert_ids * capacity + jnp.minimum(rank_pick, capacity - 1.0).astype(jnp.int32)
    back_flat = back_rows.reshape(experts * capacity, width)
    picked_rows = jnp.take(back_flat, slot_index.reshape(-1), axis=0).reshape(rows, TOP, width)
    expert_sum = jnp.sum(gate_pick[:, :, None] * picked_rows.astype(jnp.float32), axis=1)
    layer_out = (resid_mid + expert_sum).astype(jnp.bfloat16)
    dense_full = (
        lax.all_gather(attn_gain, ("dp", "fsdp"), axis=0, tiled=True),
        lax.all_gather(query_weight, ("dp", "fsdp"), axis=0, tiled=True),
        lax.all_gather(key_weight, ("dp", "fsdp"), axis=0, tiled=True),
        lax.all_gather(value_weight, ("dp", "fsdp"), axis=0, tiled=True),
        lax.all_gather(output_weight, ("dp", "fsdp"), axis=0, tiled=True),
        lax.all_gather(ffn_gain, ("dp", "fsdp"), axis=0, tiled=True),
        lax.all_gather(router_weight, ("dp", "fsdp"), axis=0, tiled=True),
    )
    expert_full = (
        lax.all_gather(expert_gate, "fsdp", axis=1, tiled=True),
        lax.all_gather(expert_up, "fsdp", axis=1, tiled=True),
        lax.all_gather(expert_down, "fsdp", axis=1, tiled=True),
    )
    gain_one, w_query, w_key, w_value, w_output, gain_two, w_router = dense_full
    w_gate, w_up, w_down = (expert_full[0][0], expert_full[1][0], expert_full[2][0])
    grad_out = out_grad.astype(jnp.float32)
    slot_gate = jnp.sum(dispatch * gates.T[:, None, :], axis=2)
    pulled_grad = jnp.einsum(
        "ecr,rd->ecd", dispatch_b, out_grad, preferred_element_type=jnp.float32
    )
    grad_send = (slot_gate[:, :, None] * pulled_grad).astype(jnp.bfloat16)
    slot_dot = jnp.sum(back_rows.astype(jnp.float32) * pulled_grad, axis=2)
    grad_gates = jnp.sum(dispatch * slot_dot[:, :, None], axis=1).T
    grad_logits = gates * (grad_gates - jnp.sum(gates * grad_gates, axis=1, keepdims=True))
    grad_logits_b = grad_logits.astype(jnp.bfloat16)
    grad_recv = lax.all_to_all(grad_send, "dp", split_axis=0, concat_axis=0, tiled=True)
    grad_rows_in, grad_gate_w, grad_up_w, grad_down_w = expert_backward(
        flat_in, gate_pre, up_pre, act_rows, grad_recv.reshape(flat_in.shape), w_gate, w_up, w_down
    )
    grad_back = lax.all_to_all(
        grad_rows_in.reshape(recv_rows.shape), "dp", split_axis=0, concat_axis=0, tiled=True
    )
    grad_routed = jnp.einsum(
        "ecr,ecd->rd", dispatch_b, grad_back, preferred_element_type=jnp.float32
    )
    grad_routed = grad_routed + jnp.dot(
        grad_logits_b, w_router.T, preferred_element_type=jnp.float32
    )
    grad_w_router = jnp.dot(routed_in.T, grad_logits_b, preferred_element_type=jnp.float32)
    grad_norm_two, grad_gain_two = norm_backward(
        grad_routed, normed_two, scale_two, gain_two.astype(jnp.float32)
    )
    grad_mid = grad_out + grad_norm_two
    grad_mid_b = grad_mid.astype(jnp.bfloat16)
    grad_w_output = jnp.dot(mixed_b.T, grad_mid_b, preferred_element_type=jnp.float32)
    grad_mixed = jnp.dot(grad_mid_b, w_output.T, preferred_element_type=jnp.float32).reshape(
        rows, KV_HEADS, groups, HEAD_DIM
    )
    grad_mixed = (grad_mixed * live_rows[:, None, None, None]).astype(jnp.bfloat16)
    probs_again, unused_total = probabilities(query_b, key_b, allowed, log_total)
    grad_probs = jnp.einsum(
        "ikgd,jkd->kgij", grad_mixed, value_b, preferred_element_type=jnp.float32
    )
    delta = jnp.sum(probs_again * grad_probs, axis=-1, keepdims=True)
    grad_scores = (probs_again * (grad_probs - delta) * scale).astype(jnp.bfloat16)
    grad_query_raw = jnp.einsum(
        "kgij,jkd->ikgd", grad_scores, key_b, preferred_element_type=jnp.float32
    )
    grad_key_raw = jnp.einsum(
        "kgij,ikgd->jkd", grad_scores, query_b, preferred_element_type=jnp.float32
    )
    grad_value_raw = jnp.einsum(
        "kgij,ikgd->jkd",
        probs_again.astype(jnp.bfloat16),
        grad_mixed,
        preferred_element_type=jnp.float32,
    )
    grad_query_b = (
        unrotate(grad_query_raw, cos_query, sin_query)
        .reshape(rows, HEADS * HEAD_DIM)
        .astype(jnp.bfloat16)
    )
    grad_key_b = (
        unrotate(grad_key_raw, cos_key, sin_key)
        .reshape(rows, KV_HEADS * HEAD_DIM)
        .astype(jnp.bfloat16)
    )
    grad_value_b = grad_value_raw.reshape(rows, KV_HEADS * HEAD_DIM).astype(jnp.bfloat16)
    grad_w_query = jnp.dot(normed_in.T, grad_query_b, preferred_element_type=jnp.float32)
    grad_w_key = jnp.dot(normed_in.T, grad_key_b, preferred_element_type=jnp.float32)
    grad_w_value = jnp.dot(normed_in.T, grad_value_b, preferred_element_type=jnp.float32)
    grad_normed = jnp.dot(grad_query_b, w_query.T, preferred_element_type=jnp.float32)
    grad_normed = grad_normed + jnp.dot(grad_key_b, w_key.T, preferred_element_type=jnp.float32)
    grad_normed = grad_normed + jnp.dot(grad_value_b, w_value.T, preferred_element_type=jnp.float32)
    grad_norm_one, grad_gain_one = norm_backward(
        grad_normed, normed_one, scale_one, gain_one.astype(jnp.float32)
    )
    grad_input = (grad_mid + grad_norm_one).astype(jnp.bfloat16)
    dense_grads = (
        lax.psum_scatter(grad_gain_one, ("dp", "fsdp"), scatter_dimension=0, tiled=True),
        lax.psum_scatter(grad_w_query, ("dp", "fsdp"), scatter_dimension=0, tiled=True),
        lax.psum_scatter(grad_w_key, ("dp", "fsdp"), scatter_dimension=0, tiled=True),
        lax.psum_scatter(grad_w_value, ("dp", "fsdp"), scatter_dimension=0, tiled=True),
        lax.psum_scatter(grad_w_output, ("dp", "fsdp"), scatter_dimension=0, tiled=True),
        lax.psum_scatter(grad_gain_two, ("dp", "fsdp"), scatter_dimension=0, tiled=True),
        lax.psum_scatter(grad_w_router, ("dp", "fsdp"), scatter_dimension=0, tiled=True),
    )
    expert_grads = (
        lax.psum_scatter(
            grad_gate_w[None].astype(jnp.bfloat16), "fsdp", scatter_dimension=1, tiled=True
        ).astype(jnp.float32),
        lax.psum_scatter(
            grad_up_w[None].astype(jnp.bfloat16), "fsdp", scatter_dimension=1, tiled=True
        ).astype(jnp.float32),
        lax.psum_scatter(
            grad_down_w[None].astype(jnp.bfloat16), "fsdp", scatter_dimension=1, tiled=True
        ).astype(jnp.float32),
    )
    return (
        layer_out,
        grad_input,
        dense_grads[0],
        dense_grads[1],
        dense_grads[2],
        dense_grads[3],
        dense_grads[4],
        dense_grads[5],
        dense_grads[6],
        expert_grads[0],
        expert_grads[1],
        expert_grads[2],
    )


def solution(mesh):
    in_specs = (
        P(("dp", "fsdp"), None),
        P(("dp", "fsdp")),
        P(("dp", "fsdp"), None),
        P(("dp", "fsdp"), None),
        P(("dp", "fsdp")),
        P(("dp", "fsdp"), None),
        P(("dp", "fsdp"), None),
        P(("dp", "fsdp"), None),
        P(("dp", "fsdp"), None),
        P(("dp", "fsdp")),
        P(("dp", "fsdp"), None),
        P("dp", "fsdp", None),
        P("dp", "fsdp", None),
        P("dp", "fsdp", None),
    )
    out_specs = (
        P(("dp", "fsdp"), None),
        P(("dp", "fsdp"), None),
        P(("dp", "fsdp")),
        P(("dp", "fsdp"), None),
        P(("dp", "fsdp"), None),
        P(("dp", "fsdp"), None),
        P(("dp", "fsdp"), None),
        P(("dp", "fsdp")),
        P(("dp", "fsdp"), None),
        P("dp", "fsdp", None),
        P("dp", "fsdp", None),
        P("dp", "fsdp", None),
    )
    return jax.shard_map(shards, mesh=mesh, in_specs=in_specs, out_specs=out_specs, check_vma=False)
```

profile of v0, /device:TPU:0, one launch (start us, length us, event | category | flops | bytes accessed | tf_op | source)
XLA Modules:
  0.0 1174.7 jit_solution(4902561280423588323)
XLA Ops:
  15.2 41.9 %all-reduce.5 = (bf16[1024]{0:T(1024)(128)(2,1)S(1)}, bf16[1024]{0:T(1024)(128)(2,1)S(1)}) all-reduce(bf16[1024]{0:T(1024)(128)(2,1)S(1)} %dynamic-update-slice, bf16[1024]{0:T(1024)(128)(2,1)S(1)} %dynamic-update-slice.1), channel_id=1, replica_groups=mesh['dp'=16,'fsdp'=2] {'dp','fsdp'}, use_global_device_ids=true, to_apply=%add | all-reduce | flops 2048 | bytes 8192
  59.3 8.2 all-gather.9.cloned.1.call-done
  67.5 1.7 convolution_convert_fusion.5
  69.3 54.0 %all-gather.11.cloned.1.call-done = bf16[1024,512]{1,0:T(8,128)(2,1)} async-done(((bf16[32,512]{1,0:T(8,128)(2,1)}), bf16[1024,512]{1,0:T(8,128)(2,1)}) %all-gather.11.cloned.1.call-update) | async-done | bytes 1048592 | tf_op jit(solution)/shard_map/all_gather | solution.py:144
  123.2 1.8 fusion.99
  125.1 56.5 %all-gather.13.cloned.1.call-done = bf16[1024,1024]{1,0:T(8,128)(2,1)} async-done(((bf16[32,1024]{1,0:T(8,128)(2,1)}), bf16[1024,1024]{1,0:T(8,128)(2,1)}) %all-gather.13.cloned.1.call-update) | async-done | bytes 2097168 | tf_op jit(solution)/shard_map/all_gather | solution.py:143
  181.6 2.6 fusion.97
  185.5 54.2 %all-gather.15.cloned.1.call-done = bf16[1024,1024]{1,0:T(8,128)(2,1)} async-done(((bf16[32,1024]{1,0:T(8,128)(2,1)}), bf16[1024,1024]{1,0:T(8,128)(2,1)}) %all-gather.15.cloned.1.call-update) | async-done | bytes 2097168 | tf_op jit(solution)/shard_map/all_gather | solution.py:146
  239.7 2.1 multiply_reduce_fusion.5
  244.0 4.5 all-to-all-start
  249.2 12.0 %all-gather.17.cloned.1.call-done = bf16[1,1024,512]{2,1,0:T(8,128)(2,1)} async-done(((bf16[1,512,512]{2,1,0:T(8,128)(2,1)}), bf16[1,1024,512]{2,1,0:T(8,128)(2,1)}) %all-gather.17.cloned.1.call-update) | async-done | bytes 1048592 | tf_op jit(solution)/shard_map/all_gather | solution.py:151
  261.2 5.9 all-to-all-done
  267.1 1.8 fusion.25
  268.9 15.0 %all-gather.19.cloned.1.call-done = bf16[1,1024,512]{2,1,0:T(8,128)(2,1)} async-done(((bf16[1,512,512]{2,1,0:T(8,128)(2,1)}), bf16[1,1024,512]{2,1,0:T(8,128)(2,1)}) %all-gather.19.cloned.1.call-update) | async-done | bytes 1048592 | tf_op jit(solution)/shard_map/all_gather | solution.py:152
  284.0 2.7 multiply_convert_fusion.3
  286.6 20.2 %all-gather.21.cloned.1.call-done = bf16[1,512,1024]{2,1,0:T(8,128)(2,1)} async-done(((bf16[1,256,1024]{2,1,0:T(8,128)(2,1)}), bf16[1,512,1024]{2,1,0:T(8,128)(2,1)}) %all-gather.21.cloned.1.call-update) | async-done | bytes 1048592 | tf_op jit(solution)/shard_map/all_gather | solution.py:153
  306.8 2.8 convolution_convert_fusion.3
  309.6 5.6 all-to-all-start.1
  315.2 76.2 %all-gather = bf16[32,32,16]{1,2,0:T(8,128)(2,1)S(1)} all-gather(bf16[1,32,16]{1,2,0:T(8,128)(2,1)S(1)} %bitcast.165), channel_id=1, replica_groups=mesh['dp'=16,'fsdp'=2] {'dp','fsdp'}, dimensions={0}, use_global_device_ids=true | all-gather | bytes 33792 | tf_op jit(solution)/shard_map/all_gather | solution.py:148
  393.6 3.6 all-to-all-start.2
  399.0 16.8 %all-to-all-done.2 = bf16[16,24,1024]{2,1,0:T(8,128)(2,1)S(1)} async-done(((bf16[16,24,1024]{2,1,0:T(8,128)(2,1)}), bf16[16,24,1024]{2,1,0:T(8,128)(2,1)S(1)}, u32[]{:S(2)}, u32[]{:S(2)}) %all-to-all-start.2) | async-done | bytes 786464 | tf_op jit(solution)/shard_map/all_to_all | solution.py:235
  415.8 2.8 multiply_convert_fusion.1
  419.4 1.7 fusion.2
  421.2 1.7 fusion.3
  423.0 1.7 fusion.23
  424.7 1.5 add_convert_fusion
  426.2 5.7 all-to-all-start.3
  433.9 4.1 gather_fusion
  438.0 2.3 multiply_reduce_fusion
  440.3 1.7 fusion.4
  442.1 8.6 all-to-all-done.3
  455.4 2.1 convolution_bitcast_fusion.4
  457.6 1.9 fusion.93
  459.6 2.1 fusion.15
  461.6 1.9 fusion.91
  463.6 2.1 convolution_bitcast_fusion.1
  465.8 2.8 fusion.95
  469.6 2.7 fusion.56
  472.3 65.3 %reduce-scatter.25.cloned.1.call-done = f32[32,16]{1,0:T(8,128)} async-done(((f32[1024,16]{1,0:T(8,128)}), f32[32,16]{1,0:T(8,128)}) %reduce-scatter.25.cloned.1.call-update) | async-done | bytes 2064
  541.4 38.1 %all-reduce.4 = (f32[1024]{0:T(1024)S(1)}, f32[1024]{0:T(1024)S(1)}) all-reduce(f32[1024]{0:T(1024)S(1)} %get-tuple-element.14, f32[1024]{0:T(1024)S(1)} %copy-done.49), channel_id=2, replica_groups=mesh['dp'=16,'fsdp'=2] {'dp','fsdp'}, use_global_device_ids=true, to_apply=%region_17.18.clone | all-reduce | flops 2048 | bytes 16384
  581.6 2.1 convert_element_type.188
  583.7 2.1 convert_element_type.191
  585.9 17.1 %reduce-scatter.23.cloned.1.call-done = bf16[1,256,1024]{2,1,0:T(8,128)(2,1)} async-done(((bf16[1,512,1024]{2,1,0:T(8,128)(2,1)}), bf16[1,256,1024]{2,1,0:T(8,128)(2,1)}) %reduce-scatter.23.cloned.1.call-update) | async-done | bytes 524304 | tf_op jit(solution)/shard_map/reduce_scatter | solution.py:314
  602.9 2.1 convert_element_type.194
  605.0 139.8 %reduce-scatter.13.cloned.1.call-done = f32[32,512]{1,0:T(8,128)} async-done(((f32[1024,512]{1,0:T(8,128)}), f32[32,512]{1,0:T(8,128)}) %reduce-scatter.13.cloned.1.call-update) | async-done | bytes 65552 | tf_op jit(solution)/shard_map/reduce_scatter | solution.py:301
  744.9 137.4 %reduce-scatter.15.cloned.1.call-done = f32[32,512]{1,0:T(8,128)} async-done(((f32[1024,512]{1,0:T(8,128)}), f32[32,512]{1,0:T(8,128)}) %reduce-scatter.15.cloned.1.call-update) | async-done | bytes 65552 | tf_op jit(solution)/shard_map/reduce_scatter | solution.py:302
  882.3 142.9 %reduce-scatter.11.cloned.1.call-done = f32[32,1024]{1,0:T(8,128)} async-done(((f32[1024,1024]{1,0:T(8,128)}), f32[32,1024]{1,0:T(8,128)}) %reduce-scatter.11.cloned.1.call-update) | async-done | bytes 131088 | tf_op jit(solution)/shard_map/reduce_scatter | solution.py:300
  1025.2 143.0 %reduce-scatter.17.cloned.1.call-done = f32[32,1024]{1,0:T(8,128)} async-done(((f32[1024,1024]{1,0:T(8,128)}), f32[32,1024]{1,0:T(8,128)}) %reduce-scatter.17.cloned.1.call-update) | async-done | bytes 131088 | tf_op jit(solution)/shard_map/reduce_scatter | solution.py:303
  (207 shorter events, 32.5 us)
Async XLA Ops:
  7.2 116.1 %copy-start = (bf16[128,1024]{1,0:T(8,128)(2,1)S(1)}, bf16[128,1024]{1,0:T(8,128)(2,1)}, u32[]{:S(2)}) copy-start(bf16[128,1024]{1,0:T(8,128)(2,1)} %param.14) | copy-start | bytes 786436
  7.2 60.3 %all-gather.9.cloned.1.call-start = ((), (), s32[]{:S(2)}) async-start(), calls=%async_computation.12 | async-start | bytes 1081344 | tf_op jit(solution)/shard_map/all_gather | solution.py:145
  7.9 115.3 %all-gather.11.cloned.1.call-start = ((), (), s32[]{:S(2)}) async-start(), calls=%async_computation.13 | async-start | bytes 1081344 | tf_op jit(solution)/shard_map/all_gather | solution.py:144
  8.7 172.9 %all-gather.13.cloned.1.call-start = ((), (), s32[]{:S(2)}) async-start(), calls=%async_computation.14 | async-start | bytes 2162688 | tf_op jit(solution)/shard_map/all_gather | solution.py:143
  9.4 230.3 %all-gather.15.cloned.1.call-start = ((), (), s32[]{:S(2)}) async-start(), calls=%async_computation.15 | async-start | bytes 2162688 | tf_op jit(solution)/shard_map/all_gather | solution.py:146
  10.0 251.3 %all-gather.17.cloned.1.call-start = ((), (), s32[]{:S(2)}) async-start(), calls=%async_computation.16 | async-start | bytes 1572864 | tf_op jit(solution)/shard_map/all_gather | solution.py:151
  10.6 273.4 %all-gather.19.cloned.1.call-start = ((), (), s32[]{:S(2)}) async-start(), calls=%async_computation.17 | async-start | bytes 1572864 | tf_op jit(solution)/shard_map/all_gather | solution.py:152
  11.8 385.4 %copy-start.55 = (f32[128]{0:T(128)}, f32[128]{0:T(128)S(1)}, u32[]{:S(2)}) copy-start(f32[128]{0:T(128)S(1)} %compare_convert_fusion) | copy-start | bytes 1540
  13.5 171.5 %copy-start.50 = (pred[128,128]{0,1:T(8,128)(4,1)}, pred[128,128]{0,1:T(8,128)(4,1)S(1)}, u32[]{:S(2)}) copy-start(pred[128,128]{0,1:T(8,128)(4,1)S(1)} %compare_and_fusion.1) | copy-start | bytes 49156
  57.1 127.1 %copy-start.29 = (f32[1024]{0:T(1024)}, f32[1024]{0:T(1024)S(1)}, u32[]{:S(2)}) copy-start(f32[1024]{0:T(1024)S(1)} %convert_element_type.150) | copy-start | bytes 12292
  58.2 126.0 %copy-start.47 = (f32[128]{0:T(128)}, f32[128]{0:T(128)S(1)}, u32[]{:S(2)}) copy-start(f32[128]{0:T(128)S(1)} %add_rsqrt_fusion.1) | copy-start | bytes 1540
  58.2 183.6 %copy-start.41 = (f32[1024]{0:T(1024)}, f32[1024]{0:T(1024)S(1)}, u32[]{:S(2)}) copy-start(f32[1024]{0:T(1024)S(1)} %convert_element_type.161) | copy-start | bytes 12292
  59.1 125.1 %copy-start.25 = (f32[128,32]{0,1:T(8,128)}, f32[128,32]{0,1:T(8,128)S(1)}, u32[]{:S(2)}) copy-start(f32[128,32]{0,1:T(8,128)S(1)} %get-tuple-element.41) | copy-start | bytes 49156
  59.2 333.1 %copy-start.39 = (f32[16,128]{1,0:T(8,128)}, f32[16,128]{1,0:T(8,128)S(1)}, u32[]{:S(2)}) copy-start(f32[16,128]{1,0:T(8,128)S(1)} %get-tuple-element.42) | copy-start | bytes 24580
  59.2 338.0 %copy-start.33 = (f32[128,16]{0,1:T(8,128)}, f32[128,16]{0,1:T(8,128)S(1)}, u32[]{:S(2)}) copy-start(f32[128,16]{0,1:T(8,128)S(1)} %get-tuple-element.43) | copy-start | bytes 24580
  69.3 115.7 %copy-start.19 = (bf16[128,512]{0,1:T(8,128)(2,1)}, bf16[128,512]{0,1:T(8,128)(2,1)S(1)}, u32[]{:S(2)}) copy-start(bf16[128,512]{0,1:T(8,128)(2,1)S(1)} %copy.69) | copy-start | bytes 393220
  125.1 59.5 %copy-start.35 = (bf16[128,8,32]{0,2,1:T(8,128)(2,1)}, bf16[128,8,32]{0,2,1:T(8,128)(2,1)S(1)}, u32[]{:S(2)}) copy-start(bf16[128,8,32]{0,2,1:T(8,128)(2,1)S(1)} %get-tuple-element.36) | copy-start | bytes 196612
  125.1 59.5 %copy-start.37 = (bf16[128,8,32]{0,2,1:T(8,128)(2,1)}, bf16[128,8,32]{0,2,1:T(8,128)(2,1)S(1)}, u32[]{:S(2)}) copy-start(bf16[128,8,32]{0,2,1:T(8,128)(2,1)S(1)} %get-tuple-element.37) | copy-start | bytes 196612
  185.0 56.9 %copy-start.13 = (f32[8,2,128,128]{2,3,1,0:T(8,128)}, f32[8,2,128,128]{2,3,1,0:T(8,128)S(1)}, u32[]{:S(2)}) copy-start(f32[8,2,128,128]{2,3,1,0:T(8,128)S(1)} %fusion.12) | copy-start | bytes 3145732
  185.5 58.5 %copy-start.16 = (bf16[8,64,2,128]{3,1,2,0:T(8,128)(2,1)}, bf16[8,64,2,128]{3,1,2,0:T(8,128)(2,1)S(1)}, u32[]{:S(2)}) copy-start(bf16[8,64,2,128]{3,1,2,0:T(8,128)(2,1)S(1)} %fusion.14) | copy-start | bytes 786436
  244.0 23.2 %all-to-all-start = ((bf16[16,24,1024]{2,1,0:T(8,128)(2,1)}), bf16[16,24,1024]{2,1,0:T(8,128)(2,1)S(1)}, u32[]{:S(2)}, u32[]{:S(2)}) async-start(bf16[16,24,1024]{2,1,0:T(8,128)(2,1)} %convolution_convert_fusion.4), calls=%async_computation | async-start | bytes 1572864 | tf_op jit(solution)/shard_map/all_to_all | solution.py:192
  248.5 58.3 %all-gather.21.cloned.1.call-start = ((), (), s32[]{:S(2)}) async-start(), calls=%async_computation.18 | async-start | bytes 1572864 | tf_op jit(solution)/shard_map/all_gather | solution.py:153
  268.9 17.7 %copy-start.18 = (f32[384,512]{1,0:T(8,128)}, f32[384,512]{1,0:T(8,128)S(1)}, u32[]{:S(2)}) copy-start(f32[384,512]{1,0:T(8,128)S(1)} %fusion.25) | copy-start | bytes 2359300
  286.6 28.6 %copy-start.27 = (bf16[384,512]{1,0:T(8,128)(2,1)}, bf16[384,512]{1,0:T(8,128)(2,1)S(1)}, u32[]{:S(2)}) copy-start(bf16[384,512]{1,0:T(8,128)(2,1)S(1)} %get-tuple-element.46) | copy-start | bytes 1179652
  286.6 28.6 %copy-start.54 = (bf16[32,16]{0,1:T(8,128)(2,1)S(1)}, bf16[32,16]{0,1:T(8,128)(2,1)}, u32[]{:S(2)}) copy-start(bf16[32,16]{0,1:T(8,128)(2,1)} %param.24) | copy-start | bytes 3076
  306.8 85.0 %copy-start.12 = (bf16[128,1024]{1,0:T(8,128)(2,1)S(1)}, bf16[128,1024]{1,0:T(8,128)(2,1)}, u32[]{:S(2)}) copy-start(bf16[128,1024]{1,0:T(8,128)(2,1)} %param.17) | copy-start | bytes 786436
  309.6 82.3 %all-to-all-start.1 = ((bf16[16,24,1024]{2,1,0:T(8,128)(2,1)}), bf16[16,24,1024]{2,1,0:T(8,128)(2,1)S(1)}, u32[]{:S(2)}, u32[]{:S(2)}) async-start(bf16[16,24,1024]{2,1,0:T(8,128)(2,1)} %bitcast.18), calls=%async_computation.1 | async-start | bytes 1572864 | tf_op jit(solution)/shard_map/all_to_all | solution.py:195
  393.6 22.3 %all-to-all-start.2 = ((bf16[16,24,1024]{2,1,0:T(8,128)(2,1)}), bf16[16,24,1024]{2,1,0:T(8,128)(2,1)S(1)}, u32[]{:S(2)}, u32[]{:S(2)}) async-start(bf16[16,24,1024]{2,1,0:T(8,128)(2,1)} %multiply_convert_fusion), calls=%async_computation.2 | async-start | bytes 1572864 | tf_op jit(solution)/shard_map/all_to_all | solution.py:235
  397.2 140.4 %reduce-scatter.25.cloned.1.call-start = ((), (), s32[]{:S(2)}) async-start(), calls=%async_computation.26 | async-start | bytes 540672
  397.9 17.9 %copy-start.43 = (bf16[128,16]{0,1:T(8,128)(2,1)}, bf16[128,16]{0,1:T(8,128)(2,1)S(1)}, u32[]{:S(2)}) copy-start(bf16[128,16]{0,1:T(8,128)(2,1)S(1)} %get-tuple-element.38) | copy-start | bytes 12292
  399.0 182.6 %reduce-scatter.19.cloned.1.call-start = ((), (), s32[]{:S(2)}) async-start(), calls=%async_computation.23 | async-start | bytes 1572864 | tf_op jit(solution)/shard_map/reduce_scatter | solution.py:308
  421.2 162.6 %reduce-scatter.21.cloned.1.call-start = ((), (), s32[]{:S(2)}) async-start(), calls=%async_computation.24 | async-start | bytes 1572864 | tf_op jit(solution)/shard_map/reduce_scatter | solution.py:311
  424.7 7.4 copy-start.14
  424.7 7.4 copy-start.51
  426.2 24.5 %all-to-all-start.3 = ((bf16[16,24,1024]{2,1,0:T(8,128)(2,1)}), bf16[16,24,1024]{2,1,0:T(8,128)(2,1)}, u32[]{:S(2)}, u32[]{:S(2)}) async-start(bf16[16,24,1024]{2,1,0:T(8,128)(2,1)} %bitcast.25), calls=%async_computation.3 | async-start | bytes 1572864 | tf_op jit(solution)/shard_map/all_to_all | solution.py:239
  432.0 170.9 %reduce-scatter.23.cloned.1.call-start = ((), (), s32[]{:S(2)}) async-start(), calls=%async_computation.25 | async-start | bytes 1572864 | tf_op jit(solution)/shard_map/reduce_scatter | solution.py:314
  440.3 10.4 copy-start.40
  440.3 11.9 %copy-start.4 = (f32[128,1024]{1,0:T(8,128)S(1)}, f32[128,1024]{1,0:T(8,128)}, u32[]{:S(2)}) copy-start(f32[128,1024]{1,0:T(8,128)} %copy-done.3) | copy-start | bytes 1572868
  440.3 11.9 %copy-start.32 = (bf16[1024,16]{0,1:T(8,128)(2,1)S(1)}, bf16[1024,16]{0,1:T(8,128)(2,1)}, u32[]{:S(2)}) copy-start(bf16[1024,16]{0,1:T(8,128)(2,1)} %copy-done.31) | copy-start | bytes 98308
  440.3 11.9 %copy-start.42 = (f32[1024]{0:T(1024)S(1)}, f32[1024]{0:T(1024)}, u32[]{:S(2)}) copy-start(f32[1024]{0:T(1024)} %copy-done.41) | copy-start | bytes 12292
  440.3 11.9 %copy-start.44 = (bf16[128,16]{0,1:T(8,128)(2,1)S(1)}, bf16[128,16]{0,1:T(8,128)(2,1)}, u32[]{:S(2)}) copy-start(bf16[128,16]{0,1:T(8,128)(2,1)} %copy-done.43) | copy-start | bytes 12292
  440.3 11.9 %copy-start.53 = (f32[128]{0:T(128)S(1)}, f32[128]{0:T(128)}, u32[]{:S(2)}) copy-start(f32[128]{0:T(128)} %copy-done.52) | copy-start | bytes 1540
  442.0 11.1 copy-start.10
  442.1 302.8 %reduce-scatter.13.cloned.1.call-start = ((), (), s32[]{:S(2)}) async-start(), calls=%async_computation.20 | async-start | bytes 2162688 | tf_op jit(solution)/shard_map/reduce_scatter | solution.py:301
  459.5 422.8 %reduce-scatter.15.cloned.1.call-start = ((), (), s32[]{:S(2)}) async-start(), calls=%async_computation.21 | async-start | bytes 2162688 | tf_op jit(solution)/shard_map/reduce_scatter | solution.py:302
  463.5 561.6 %reduce-scatter.11.cloned.1.call-start = ((), (), s32[]{:S(2)}) async-start(), calls=%async_computation.19 | async-start | bytes 4325376 | tf_op jit(solution)/shard_map/reduce_scatter | solution.py:300
  468.6 699.5 %reduce-scatter.17.cloned.1.call-start = ((), (), s32[]{:S(2)}) async-start(), calls=%async_computation.22 | async-start | bytes 4325376 | tf_op jit(solution)/shard_map/reduce_scatter | solution.py:303
  472.3 66.7 %copy-start.1 = (bf16[1024,1024]{1,0:T(8,128)(2,1)S(1)}, bf16[1024,1024]{1,0:T(8,128)(2,1)}, u32[]{:S(2)}) copy-start(bf16[1024,1024]{1,0:T(8,128)(2,1)} %all-gather.13.cloned.1.call-done) | copy-start | bytes 6291460
  (28 other events, 62.5 us)
Sparse Core Ops, SparseCore 0:
  10.9 56.5 all-gather.8
  70.4 52.8 all-gather.10
  126.2 55.3 all-gather.12
  184.4 55.1 all-gather.14
  241.1 20.1 all-gather.16
  262.6 21.2 all-gather.18
  285.5 21.2 all-gather.20
  400.3 137.3 reduce-scatter.24
  540.4 17.0 reduce-scatter.18
  559.6 20.5 reduce-scatter.20
  582.4 20.4 reduce-scatter.22
  605.6 139.2 reduce-scatter.12
  747.7 134.5 reduce-scatter.14
  885.0 140.1 reduce-scatter.10
  1027.9 140.2 reduce-scatter.16
where the time goes:
time: 1180 us; the launch traced here: 1170 us
  waiting for transfers between devices  901 us (76%)
  blocking collectives  156 us (13%)
  matrix products  51.4 us (4%)
  starting transfers between devices  20 us (2%)
  other arithmetic  18.5 us (2%)
  between operations  14.8 us (1%)
  local copies, waits for them, and re-layouts  12.5 us (1%)
    reduce_scatter x1, waiting for transfers between devices, shards(): lax.psum_scatter(grad_w_output, ('dp', 'fsdp'), scatter_dimension=0, tile...  143 us
    reduce_scatter x1, waiting for transfers between devices, shards(): lax.psum_scatter(grad_w_query, ('dp', 'fsdp'), scatter_dimension=0, tiled...  143 us
    reduce_scatter x1, waiting for transfers between devices, shards(): lax.psum_scatter(grad_w_key, ('dp', 'fsdp'), scatter_dimension=0, tiled=T...  140 us
    reduce_scatter x1, waiting for transfers between devices, shards(): lax.psum_scatter(grad_w_value, ('dp', 'fsdp'), scatter_dimension=0, tiled...  137 us
    unnamed x2, blocking collectives  80 us
    all_gather x1, blocking collectives, shards(): lax.all_gather(router_weight, ('dp', 'fsdp'), axis=0, tiled=True)  76.2 us
    unnamed x16, waiting for transfers between devices  69.8 us
    all_gather x1, waiting for transfers between devices, shards(): lax.all_gather(query_weight, ('dp', 'fsdp'), axis=0, tiled=True)  56.5 us
  transfers between devices with their start and end apart: 19, of which 16 were waited for; matrix products, arithmetic and copies ran while one was open for 6% of the time, Pallas kernels for 0%

commit v1 on v0

--- a/solution.py
+++ b/solution.py
@@ -9,6 +9,13 @@
 TOP = 8
 CAP = 24
 norm_eps = 1e-05
+
+
+def all_by_exchange(x, axis, d):
+    devices = lax.axis_size(axis)
+    shards = jnp.stack([x for _ in range(devices)])
+    shards = lax.all_to_all(shards, axis, split_axis=0, concat_axis=0)
+    return jnp.concatenate(shards, axis=d)
 
 
 def positions_mask(doc_block):
@@ -145,7 +152,7 @@
         lax.all_gather(value_weight, ("dp", "fsdp"), axis=0, tiled=True),
         lax.all_gather(output_weight, ("dp", "fsdp"), axis=0, tiled=True),
         lax.all_gather(ffn_gain, ("dp", "fsdp"), axis=0, tiled=True),
-        lax.all_gather(router_weight, ("dp", "fsdp"), axis=0, tiled=True),
+        all_by_exchange(router_weight, ("dp", "fsdp"), 0),
     )
     expert_full = (
         lax.all_gather(expert_gate, "fsdp", axis=1, tiled=True),

time: 1180 us -> 1120 us (0.949)
  waiting for transfers between devices: 901 us -> 842 us
    unnamed x16, waiting for transfers between devices: 69.8 us -> 4.48 us
    all_to_all x1, waiting for transfers between devices: 0.01 us -> 18.1 us  [shards(): lax.all_to_all(out_rows.reshape(recv_rows.shape), 'dp', split_axis=0, con...]
    all_gather x1, waiting for transfers between devices: 12 us -> 0.02 us  [shards(): lax.all_gather(expert_gate, 'fsdp', axis=1, tiled=True)]
  transfers between devices with their start and end apart: 19 -> 20, of which waited for: 16 -> 15; matrix products, arithmetic and copies ran while one was open for 6% -> 7% of each run, Pallas kernels for 0% -> 0%
where the time goes in v1:
time: 1120 us
  waiting for transfers between devices  842 us (75%)
  blocking collectives  151 us (13%)
  matrix products  51.4 us (5%)
  starting transfers between devices  24.9 us (2%)
  other arithmetic  18.5 us (2%)
  local copies, waits for them, and re-layouts  15.9 us (1%)
  between operations  14.8 us (1%)
    reduce_scatter x1, waiting for transfers between devices, shards(): lax.psum_scatter(grad_w_output, ('dp', 'fsdp'), scatter_dimension=0, tile...  143 us
    reduce_scatter x1, waiting for transfers between devices, shards(): lax.psum_scatter(grad_w_query, ('dp', 'fsdp'), scatter_dimension=0, tiled...  143 us
    reduce_scatter x1, waiting for transfers between devices, shards(): lax.psum_scatter(grad_w_key, ('dp', 'fsdp'), scatter_dimension=0, tiled=T...  140 us
    reduce_scatter x1, waiting for transfers between devices, shards(): lax.psum_scatter(grad_w_value, ('dp', 'fsdp'), scatter_dimension=0, tiled...  138 us
    unnamed x2, blocking collectives  82.6 us
    all_gather x1, blocking collectives, shards(): lax.all_gather(router_weight, ('dp', 'fsdp'), axis=0, tiled=True)  68.6 us
    all_gather x1, waiting for transfers between devices, shards(): lax.all_gather(query_weight, ('dp', 'fsdp'), axis=0, tiled=True)  56.5 us
    all_gather x1, waiting for transfers between devices, shards(): lax.all_gather(output_weight, ('dp', 'fsdp'), axis=0, tiled=True)  54.2 us
  transfers between devices with their start and end apart: 20, of which 15 were waited for; matrix products, arithmetic and copies ran while one was open for 7% of the time, Pallas kernels for 0%

profile of v1, /device:TPU:0, one launch (start us, length us, event | category | flops | bytes accessed | tf_op | source)
XLA Modules:
  0.0 1118.7 jit_solution(4562393542180636791)
XLA Ops:
  15.2 41.9 %all-reduce.5 = (bf16[1024]{0:T(1024)(128)(2,1)S(1)}, bf16[1024]{0:T(1024)(128)(2,1)S(1)}) all-reduce(bf16[1024]{0:T(1024)(128)(2,1)S(1)} %dynamic-update-slice, bf16[1024]{0:T(1024)(128)(2,1)S(1)} %dynamic-update-slice.1), channel_id=1, replica_groups=mesh['dp'=16,'fsdp'=2] {'dp','fsdp'}, use_global_device_ids=true, to_apply=%add | all-reduce | flops 2048 | bytes 8192
  59.3 8.2 all-gather.9.cloned.1.call-done
  67.5 1.7 convolution_convert_fusion.5
  69.3 54.0 %all-gather.11.cloned.1.call-done = bf16[1024,512]{1,0:T(8,128)(2,1)} async-done(((bf16[32,512]{1,0:T(8,128)(2,1)}), bf16[1024,512]{1,0:T(8,128)(2,1)}) %all-gather.11.cloned.1.call-update) | async-done | bytes 1048592 | tf_op jit(solution)/shard_map/all_gather | solution.py:151
  123.2 1.8 fusion.99
  125.1 56.5 %all-gather.13.cloned.1.call-done = bf16[1024,1024]{1,0:T(8,128)(2,1)} async-done(((bf16[32,1024]{1,0:T(8,128)(2,1)}), bf16[1024,1024]{1,0:T(8,128)(2,1)}) %all-gather.13.cloned.1.call-update) | async-done | bytes 2097168 | tf_op jit(solution)/shard_map/all_gather | solution.py:150
  181.6 2.6 fusion.97
  185.5 54.2 %all-gather.15.cloned.1.call-done = bf16[1024,1024]{1,0:T(8,128)(2,1)} async-done(((bf16[32,1024]{1,0:T(8,128)(2,1)}), bf16[1024,1024]{1,0:T(8,128)(2,1)}) %all-gather.15.cloned.1.call-update) | async-done | bytes 2097168 | tf_op jit(solution)/shard_map/all_gather | solution.py:153
  239.7 2.1 multiply_reduce_fusion.5
  244.0 4.5 all-to-all-start.1
  250.0 17.1 %all-to-all-done.1 = bf16[16,24,1024]{2,1,0:T(8,128)(2,1)S(1)} async-done(((bf16[16,24,1024]{2,1,0:T(8,128)(2,1)}), bf16[16,24,1024]{2,1,0:T(8,128)(2,1)S(1)}, u32[]{:S(2)}, u32[]{:S(2)}) %all-to-all-start.1) | async-done | bytes 786464 | tf_op jit(solution)/shard_map/all_to_all | solution.py:199
  267.2 4.4 all-to-all-start
  271.6 1.8 fusion.25
  273.4 10.9 all-gather.19.cloned.1.call-done
  284.3 2.7 multiply_convert_fusion.3
  287.0 20.2 %all-gather.21.cloned.1.call-done = bf16[1,512,1024]{2,1,0:T(8,128)(2,1)} async-done(((bf16[1,256,1024]{2,1,0:T(8,128)(2,1)}), bf16[1,512,1024]{2,1,0:T(8,128)(2,1)}) %all-gather.21.cloned.1.call-update) | async-done | bytes 1048592 | tf_op jit(solution)/shard_map/all_gather | solution.py:160
  307.2 2.7 convolution_convert_fusion.3
  309.9 5.6 all-to-all-start.2
  316.1 18.1 %all-to-all-done.2 = bf16[16,24,1024]{2,1,0:T(8,128)(2,1)S(1)} async-done(((bf16[16,24,1024]{2,1,0:T(8,128)(2,1)}), bf16[16,24,1024]{2,1,0:T(8,128)(2,1)S(1)}, u32[]{:S(2)}, u32[]{:S(2)}) %all-to-all-start.2) | async-done | bytes 786464 | tf_op jit(solution)/shard_map/all_to_all | solution.py:202
  335.9 5.4 all-to-all-start.3
  343.1 16.8 %all-to-all-done.3 = bf16[16,24,1024]{2,1,0:T(8,128)(2,1)S(1)} async-done(((bf16[16,24,1024]{2,1,0:T(8,128)(2,1)}), bf16[16,24,1024]{2,1,0:T(8,128)(2,1)S(1)}, u32[]{:S(2)}, u32[]{:S(2)}) %all-to-all-start.3) | async-done | bytes 786464 | tf_op jit(solution)/shard_map/all_to_all | solution.py:242
  360.0 2.8 multiply_convert_fusion.1
  363.5 1.7 fusion.2
  365.3 68.6 %all-gather = bf16[32,32,16]{1,2,0:T(8,128)(2,1)S(1)} all-gather(bf16[1,32,16]{1,2,0:T(8,128)(2,1)} %bitcast.170), channel_id=1, replica_groups=mesh['dp'=16,'fsdp'=2] {'dp','fsdp'}, dimensions={0}, use_global_device_ids=true | all-gather | bytes 33792 | tf_op jit(solution)/shard_map/all_gather | solution.py:223
  434.6 1.7 reshape.309
  436.3 1.7 fusion.3
  438.1 1.7 fusion.23
  441.3 4.4 all-to-all-start.4
  447.7 4.1 gather_fusion
  451.8 2.3 multiply_reduce_fusion
  454.1 1.7 fusion.4
  455.9 8.6 all-to-all-done.4
  469.2 2.1 convolution_bitcast_fusion.4
  471.4 1.9 fusion.93
  473.3 2.1 fusion.15
  475.5 1.8 fusion.91
  477.4 2.1 convolution_bitcast_fusion.1
  479.6 2.8 fusion.95
  483.4 2.7 fusion.56
  490.0 40.7 %all-reduce.4 = (f32[1024]{0:T(1024)S(1)}, f32[1024]{0:T(1024)S(1)}) all-reduce(f32[1024]{0:T(1024)S(1)} %get-tuple-element.14, f32[1024]{0:T(1024)S(1)} %copy-done.48), channel_id=2, replica_groups=mesh['dp'=16,'fsdp'=2] {'dp','fsdp'}, use_global_device_ids=true, to_apply=%region_17.18.clone | all-reduce | flops 2048 | bytes 16384
  532.8 2.1 convert_element_type.188
  535.0 2.1 convert_element_type.191
  537.1 9.2 reduce-scatter.23.cloned.1.call-done
  546.4 2.1 convert_element_type.194
  548.5 139.7 %reduce-scatter.13.cloned.1.call-done = f32[32,512]{1,0:T(8,128)} async-done(((f32[1024,512]{1,0:T(8,128)}), f32[32,512]{1,0:T(8,128)}) %reduce-scatter.13.cloned.1.call-update) | async-done | bytes 65552 | tf_op jit(solution)/shard_map/reduce_scatter | solution.py:308
  688.2 138.0 %reduce-scatter.15.cloned.1.call-done = f32[32,512]{1,0:T(8,128)} async-done(((f32[1024,512]{1,0:T(8,128)}), f32[32,512]{1,0:T(8,128)}) %reduce-scatter.15.cloned.1.call-update) | async-done | bytes 65552 | tf_op jit(solution)/shard_map/reduce_scatter | solution.py:309
  826.2 142.7 %reduce-scatter.11.cloned.1.call-done = f32[32,1024]{1,0:T(8,128)} async-done(((f32[1024,1024]{1,0:T(8,128)}), f32[32,1024]{1,0:T(8,128)}) %reduce-scatter.11.cloned.1.call-update) | async-done | bytes 131088 | tf_op jit(solution)/shard_map/reduce_scatter | solution.py:307
  969.0 143.2 %reduce-scatter.17.cloned.1.call-done = f32[32,1024]{1,0:T(8,128)} async-done(((f32[1024,1024]{1,0:T(8,128)}), f32[32,1024]{1,0:T(8,128)}) %reduce-scatter.17.cloned.1.call-update) | async-done | bytes 131088 | tf_op jit(solution)/shard_map/reduce_scatter | solution.py:310
  (212 shorter events, 35.9 us)
Async XLA Ops:
  7.2 116.1 %copy-start = (bf16[128,1024]{1,0:T(8,128)(2,1)S(1)}, bf16[128,1024]{1,0:T(8,128)(2,1)}, u32[]{:S(2)}) copy-start(bf16[128,1024]{1,0:T(8,128)(2,1)} %param.14) | copy-start | bytes 786436
  7.2 60.3 %all-gather.9.cloned.1.call-start = ((), (), s32[]{:S(2)}) async-start(), calls=%async_computation.13 | async-start | bytes 1081344 | tf_op jit(solution)/shard_map/all_gather | solution.py:152
  7.9 115.3 %all-gather.11.cloned.1.call-start = ((), (), s32[]{:S(2)}) async-start(), calls=%async_computation.14 | async-start | bytes 1081344 | tf_op jit(solution)/shard_map/all_gather | solution.py:151
  8.7 172.9 %all-gather.13.cloned.1.call-start = ((), (), s32[]{:S(2)}) async-start(), calls=%async_computation.15 | async-start | bytes 2162688 | tf_op jit(solution)/shard_map/all_gather | solution.py:150
  9.4 230.3 %all-gather.15.cloned.1.call-start = ((), (), s32[]{:S(2)}) async-start(), calls=%async_computation.16 | async-start | bytes 2162688 | tf_op jit(solution)/shard_map/all_gather | solution.py:153
  10.0 261.6 %all-gather.17.cloned.1.call-start = ((), (), s32[]{:S(2)}) async-start(), calls=%async_computation.17 | async-start | bytes 1572864 | tf_op jit(solution)/shard_map/all_gather | solution.py:158
  10.6 273.7 %all-gather.19.cloned.1.call-start = ((), (), s32[]{:S(2)}) async-start(), calls=%async_computation.18 | async-start | bytes 1572864 | tf_op jit(solution)/shard_map/all_gather | solution.py:159
  11.8 329.5 %copy-start.54 = (f32[128]{0:T(128)}, f32[128]{0:T(128)S(1)}, u32[]{:S(2)}) copy-start(f32[128]{0:T(128)S(1)} %compare_convert_fusion) | copy-start | bytes 1540
  13.5 171.5 %copy-start.50 = (pred[128,128]{0,1:T(8,128)(4,1)}, pred[128,128]{0,1:T(8,128)(4,1)S(1)}, u32[]{:S(2)}) copy-start(pred[128,128]{0,1:T(8,128)(4,1)S(1)} %compare_and_fusion.1) | copy-start | bytes 49156
  57.1 127.0 %copy-start.29 = (f32[1024]{0:T(1024)}, f32[1024]{0:T(1024)S(1)}, u32[]{:S(2)}) copy-start(f32[1024]{0:T(1024)S(1)} %convert_element_type.150) | copy-start | bytes 12292
  58.2 126.0 %copy-start.46 = (f32[128]{0:T(128)}, f32[128]{0:T(128)S(1)}, u32[]{:S(2)}) copy-start(f32[128]{0:T(128)S(1)} %add_rsqrt_fusion.1) | copy-start | bytes 1540
  58.2 183.6 %copy-start.40 = (f32[1024]{0:T(1024)}, f32[1024]{0:T(1024)S(1)}, u32[]{:S(2)}) copy-start(f32[1024]{0:T(1024)S(1)} %convert_element_type.161) | copy-start | bytes 12292
  59.1 125.1 %copy-start.25 = (f32[128,32]{0,1:T(8,128)}, f32[128,32]{0,1:T(8,128)S(1)}, u32[]{:S(2)}) copy-start(f32[128,32]{0,1:T(8,128)S(1)} %get-tuple-element.41) | copy-start | bytes 49156
  59.2 275.4 %copy-start.38 = (f32[16,128]{1,0:T(8,128)}, f32[16,128]{1,0:T(8,128)S(1)}, u32[]{:S(2)}) copy-start(f32[16,128]{1,0:T(8,128)S(1)} %get-tuple-element.42) | copy-start | bytes 24580
  59.2 282.1 %copy-start.31 = (f32[128,16]{0,1:T(8,128)}, f32[128,16]{0,1:T(8,128)S(1)}, u32[]{:S(2)}) copy-start(f32[128,16]{0,1:T(8,128)S(1)} %get-tuple-element.43) | copy-start | bytes 24580
  69.3 115.7 %copy-start.19 = (bf16[128,512]{0,1:T(8,128)(2,1)}, bf16[128,512]{0,1:T(8,128)(2,1)S(1)}, u32[]{:S(2)}) copy-start(bf16[128,512]{0,1:T(8,128)(2,1)S(1)} %copy.86) | copy-start | bytes 393220
  125.1 59.5 %copy-start.33 = (bf16[128,8,32]{0,2,1:T(8,128)(2,1)}, bf16[128,8,32]{0,2,1:T(8,128)(2,1)S(1)}, u32[]{:S(2)}) copy-start(bf16[128,8,32]{0,2,1:T(8,128)(2,1)S(1)} %get-tuple-element.36) | copy-start | bytes 196612
  125.1 59.5 %copy-start.35 = (bf16[128,8,32]{0,2,1:T(8,128)(2,1)}, bf16[128,8,32]{0,2,1:T(8,128)(2,1)S(1)}, u32[]{:S(2)}) copy-start(bf16[128,8,32]{0,2,1:T(8,128)(2,1)S(1)} %get-tuple-element.37) | copy-start | bytes 196612
  185.0 56.8 %copy-start.13 = (f32[8,2,128,128]{2,3,1,0:T(8,128)}, f32[8,2,128,128]{2,3,1,0:T(8,128)S(1)}, u32[]{:S(2)}) copy-start(f32[8,2,128,128]{2,3,1,0:T(8,128)S(1)} %fusion.12) | copy-start | bytes 3145732
  185.5 58.5 %copy-start.16 = (bf16[8,64,2,128]{3,1,2,0:T(8,128)(2,1)}, bf16[8,64,2,128]{3,1,2,0:T(8,128)(2,1)S(1)}, u32[]{:S(2)}) copy-start(bf16[8,64,2,128]{3,1,2,0:T(8,128)(2,1)S(1)} %fusion.14) | copy-start | bytes 786436
  241.8 7.4 copy-start.49
  244.0 23.2 %all-to-all-start.1 = ((bf16[16,24,1024]{2,1,0:T(8,128)(2,1)}), bf16[16,24,1024]{2,1,0:T(8,128)(2,1)S(1)}, u32[]{:S(2)}, u32[]{:S(2)}) async-start(bf16[16,24,1024]{2,1,0:T(8,128)(2,1)} %convolution_convert_fusion.4), calls=%async_computation.1 | async-start | bytes 1572864 | tf_op jit(solution)/shard_map/all_to_all | solution.py:199
  248.5 58.7 %all-gather.21.cloned.1.call-start = ((), (), s32[]{:S(2)}) async-start(), calls=%async_computation.19 | async-start | bytes 1572864 | tf_op jit(solution)/shard_map/all_gather | solution.py:160
  267.2 42.8 %all-to-all-start = ((bf16[32,2,256]{2,1,0:T(2,128)(2,1)}), bf16[32,2,256]{2,1,0:T(2,128)(2,1)S(1)}, u32[]{:S(2)}, u32[]{:S(2)}) async-start(bf16[32,2,256]{2,1,0:T(2,128)(2,1)} %reshape.319), calls=%async_computation | async-start | bytes 65536 | tf_op jit(solution)/shard_map/all_to_all | solution.py:17
  273.3 13.6 %copy-start.18 = (f32[384,512]{1,0:T(8,128)}, f32[384,512]{1,0:T(8,128)S(1)}, u32[]{:S(2)}) copy-start(f32[384,512]{1,0:T(8,128)S(1)} %fusion.25) | copy-start | bytes 2359300
  287.0 22.9 %copy-start.27 = (bf16[384,512]{1,0:T(8,128)(2,1)}, bf16[384,512]{1,0:T(8,128)(2,1)S(1)}, u32[]{:S(2)}) copy-start(bf16[384,512]{1,0:T(8,128)(2,1)S(1)} %get-tuple-element.46) | copy-start | bytes 1179652
  307.2 27.1 %copy-start.12 = (bf16[128,1024]{1,0:T(8,128)(2,1)S(1)}, bf16[128,1024]{1,0:T(8,128)(2,1)}, u32[]{:S(2)}) copy-start(bf16[128,1024]{1,0:T(8,128)(2,1)} %param.17) | copy-start | bytes 786436
  309.9 24.3 %all-to-all-start.2 = ((bf16[16,24,1024]{2,1,0:T(8,128)(2,1)}), bf16[16,24,1024]{2,1,0:T(8,128)(2,1)S(1)}, u32[]{:S(2)}, u32[]{:S(2)}) async-start(bf16[16,24,1024]{2,1,0:T(8,128)(2,1)} %bitcast.17), calls=%async_computation.2 | async-start | bytes 1572864 | tf_op jit(solution)/shard_map/all_to_all | solution.py:202
  335.9 24.1 %all-to-all-start.3 = ((bf16[16,24,1024]{2,1,0:T(8,128)(2,1)}), bf16[16,24,1024]{2,1,0:T(8,128)(2,1)S(1)}, u32[]{:S(2)}, u32[]{:S(2)}) async-start(bf16[16,24,1024]{2,1,0:T(8,128)(2,1)} %multiply_convert_fusion), calls=%async_computation.3 | async-start | bytes 1572864 | tf_op jit(solution)/shard_map/all_to_all | solution.py:242
  341.3 144.8 %reduce-scatter.25.cloned.1.call-start = ((), (), s32[]{:S(2)}) async-start(), calls=%async_computation.27 | async-start | bytes 540672
  342.0 18.0 %copy-start.42 = (bf16[128,16]{0,1:T(8,128)(2,1)}, bf16[128,16]{0,1:T(8,128)(2,1)S(1)}, u32[]{:S(2)}) copy-start(bf16[128,16]{0,1:T(8,128)(2,1)S(1)} %get-tuple-element.38) | copy-start | bytes 12292
  343.1 189.8 %reduce-scatter.19.cloned.1.call-start = ((), (), s32[]{:S(2)}) async-start(), calls=%async_computation.24 | async-start | bytes 1572864 | tf_op jit(solution)/shard_map/reduce_scatter | solution.py:315
  365.3 72.8 %copy-start.5 = (bf16[1,1024,512]{2,1,0:T(8,128)(2,1)S(1)}, bf16[1,1024,512]{2,1,0:T(8,128)(2,1)}, u32[]{:S(2)}) copy-start(bf16[1,1024,512]{2,1,0:T(8,128)(2,1)} %all-gather.17.cloned.1.call-done) | copy-start | bytes 3145732
  365.3 169.7 %reduce-scatter.21.cloned.1.call-start = ((), (), s32[]{:S(2)}) async-start(), calls=%async_computation.25 | async-start | bytes 1572864 | tf_op jit(solution)/shard_map/reduce_scatter | solution.py:318
  439.8 6.1 copy-start.14
  441.3 23.1 %all-to-all-start.4 = ((bf16[16,24,1024]{2,1,0:T(8,128)(2,1)}), bf16[16,24,1024]{2,1,0:T(8,128)(2,1)}, u32[]{:S(2)}, u32[]{:S(2)}) async-start(bf16[16,24,1024]{2,1,0:T(8,128)(2,1)} %bitcast.24), calls=%async_computation.4 | async-start | bytes 1572864 | tf_op jit(solution)/shard_map/all_to_all | solution.py:246
  445.8 100.6 %reduce-scatter.23.cloned.1.call-start = ((), (), s32[]{:S(2)}) async-start(), calls=%async_computation.26 | async-start | bytes 1572864 | tf_op jit(solution)/shard_map/reduce_scatter | solution.py:321
  454.1 10.4 copy-start.39
  454.1 11.9 %copy-start.4 = (f32[128,1024]{1,0:T(8,128)S(1)}, f32[128,1024]{1,0:T(8,128)}, u32[]{:S(2)}) copy-start(f32[128,1024]{1,0:T(8,128)} %copy-done.3) | copy-start | bytes 1572868
  454.1 11.9 %copy-start.37 = (bf16[1024,16]{0,1:T(8,128)(2,1)S(1)}, bf16[1024,16]{0,1:T(8,128)(2,1)}, u32[]{:S(2)}) copy-start(bf16[1024,16]{0,1:T(8,128)(2,1)} %reshape.309) | copy-start | bytes 98308
  454.1 11.9 %copy-start.41 = (f32[1024]{0:T(1024)S(1)}, f32[1024]{0:T(1024)}, u32[]{:S(2)}) copy-start(f32[1024]{0:T(1024)} %copy-done.40) | copy-start | bytes 12292
  454.1 11.9 %copy-start.43 = (bf16[128,16]{0,1:T(8,128)(2,1)S(1)}, bf16[128,16]{0,1:T(8,128)(2,1)}, u32[]{:S(2)}) copy-start(bf16[128,16]{0,1:T(8,128)(2,1)} %copy-done.42) | copy-start | bytes 12292
  454.1 11.9 %copy-start.53 = (f32[128]{0:T(128)S(1)}, f32[128]{0:T(128)}, u32[]{:S(2)}) copy-start(f32[128]{0:T(128)} %copy-done.52) | copy-start | bytes 1540
  455.8 11.1 copy-start.10
  455.9 232.4 %reduce-scatter.13.cloned.1.call-start = ((), (), s32[]{:S(2)}) async-start(), calls=%async_computation.21 | async-start | bytes 2162688 | tf_op jit(solution)/shard_map/reduce_scatter | solution.py:308
  473.3 352.9 %reduce-scatter.15.cloned.1.call-start = ((), (), s32[]{:S(2)}) async-start(), calls=%async_computation.22 | async-start | bytes 2162688 | tf_op jit(solution)/shard_map/reduce_scatter | solution.py:309
  477.3 491.6 %reduce-scatter.11.cloned.1.call-start = ((), (), s32[]{:S(2)}) async-start(), calls=%async_computation.20 | async-start | bytes 4325376 | tf_op jit(solution)/shard_map/reduce_scatter | solution.py:307
  482.4 629.7 %reduce-scatter.17.cloned.1.call-start = ((), (), s32[]{:S(2)}) async-start(), calls=%async_computation.23 | async-start | bytes 4325376 | tf_op jit(solution)/shard_map/reduce_scatter | solution.py:310
  (28 other events, 62.5 us)
Sparse Core Ops, SparseCore 0:
  10.9 56.5 all-gather.8
  70.4 52.8 all-gather.10
  126.2 55.3 all-gather.12
  184.4 55.1 all-gather.14
  241.1 20.1 all-gather.16
  262.6 21.6 all-gather.18
  285.8 21.2 all-gather.20
  344.4 136.7 reduce-scatter.24
  484.0 16.9 reduce-scatter.18
  503.1 20.5 reduce-scatter.20
  525.9 20.4 reduce-scatter.22
  549.1 139.1 reduce-scatter.12
  691.1 135.1 reduce-scatter.14
  829.0 139.9 reduce-scatter.10
  971.6 140.4 reduce-scatter.16
